TPU v7x, 128 devices: a whole 4x4x4 slice. The times are simulated.
128 devices in a mesh: row: 8 (over y, core), col: 16 (over x, z).
Axes of the slice: x: 4, y: 4, z: 4, core: 2. Of those that a mesh axis runs over, the one named last changes fastest.
Arguments:
- features: bfloat16 [262144, 128], P(('row', 'col')), may hold values from -6 to 6
- new_index: int32 [262144], P(('row', 'col')), may hold values from 0 to 262143, as said below
- tile_values: bfloat16 [8, 16, 640, 128, 128], P('row', 'col'), may hold values from -0.125 to 0.125
- tile_index: int32 [8, 16, 2, 640], P('row', 'col'), may hold values from 0 to 255, as said below
- tile_count: int32 [8, 16], P('row', 'col'), may hold values from 80 to 640, as said below
- weight: bfloat16 [128, 256], replicated, may hold values from -0.5 to 0.5
- bias: float32 [256], replicated, may hold values from -3 to 3
Outputs:
- hidden: bfloat16 [262144, 256], P(('row', 'col'))
Inputs may be any that keep to these rules, and one draw needn't show every extreme that they name: A permutation. The new owner of a vertex is k = new_index // 2048; owner k is the device at grid row k mod the number of grid rows and grid column k div that number. From one device to one new owner at most 32 vertices move, and exactly 32 do for some pair in every draw. `tile_index`: entry 0 of a slot is a row tile below 256, entry 1 a column tile below 128; the slots of one grid block name distinct tiles. `tile_count`: some grid block holds 640 nonzero tiles in every draw.
All inputs are finite; a program needn't handle non-finite values.
Results may differ from a plain program's by a relative error of at most 0.017.
Values may be sent and summed in bfloat16 or wider, within the bound.
No kernel may reach another device: no remote copies, remote signals or barrier semaphores. Data moves between devices by JAX's collectives and lax.ppermute only.
A program may use at most 128 MiB of HBM per device.

v0:
```python
import jax
import jax.numpy as jnp
from jax import lax
from jax.sharding import PartitionSpec as P

GROUP = 64


def body(features, new_index, tile_values, tile_index, tile_count, weight, bias):
    grid_rows = lax.axis_size("row")
    grid_cols = lax.axis_size("col")
    device_total = grid_rows * grid_cols
    local_rows = features.shape[0]
    feature_width = features.shape[1]
    capacity = 2 * local_rows // device_total
    new_owner = new_index // local_rows
    new_slot = new_index % local_rows
    target_peer = new_owner % grid_rows * grid_cols + new_owner // grid_rows
    peer_hits = (target_peer[:, None] == jnp.arange(device_total, dtype=jnp.int32)[None, :]).astype(
        jnp.int32
    )
    peer_rank = jnp.sum((jnp.cumsum(peer_hits, axis=0) - peer_hits) * peer_hits, axis=1)
    outgoing = (
        jnp.zeros((device_total, capacity, feature_width), jnp.bfloat16)
        .at[target_peer, peer_rank]
        .set(features)
    )
    slots_out = (
        jnp.full((device_total, capacity), local_rows, jnp.int32)
        .at[target_peer, peer_rank]
        .set(new_slot)
    )
    rows_in, slots_in = (
        lax.all_to_all(outgoing, ("row", "col"), split_axis=0, concat_axis=0, tiled=True),
        lax.all_to_all(slots_out, ("row", "col"), split_axis=0, concat_axis=0, tiled=True),
    )
    moved_rows = (
        jnp.zeros((local_rows, feature_width), jnp.bfloat16)
        .at[slots_in.reshape(-1)]
        .set(rows_in.reshape(-1, feature_width), mode="drop")
    )
    column_block = lax.all_gather(moved_rows, "row", axis=0, tiled=True)
    tile_set = tile_values[0, 0]
    tile_coords = tile_index[0, 0]
    tile_total = tile_count[0, 0]
    tile_edge = tile_set.shape[1]
    col_tiles = column_block.shape[0] // tile_edge
    row_tiles = local_rows * grid_cols // tile_edge
    input_tiles = column_block.reshape(col_tiles, tile_edge, feature_width)

    def add_tiles(step_index, totals):
        first_tile = step_index * GROUP
        part_tiles = lax.dynamic_slice_in_dim(tile_set, first_tile, GROUP, 0)
        part_rows = lax.dynamic_slice_in_dim(tile_coords[0], first_tile, GROUP, 0)
        part_cols = lax.dynamic_slice_in_dim(tile_coords[1], first_tile, GROUP, 0)
        inputs = input_tiles[part_cols]
        products = jnp.einsum(
            "tab,tbf->taf", part_tiles, inputs, preferred_element_type=jnp.float32
        )
        live_mask = first_tile + jnp.arange(GROUP, dtype=jnp.int32) < tile_total
        products = jnp.where(live_mask[:, None, None], products, jnp.zeros_like(products))
        return totals.at[part_rows].add(products)

    trips = (tile_total + GROUP - 1) // GROUP
    totals = lax.fori_loop(
        0, trips, add_tiles, jnp.zeros((row_tiles, tile_edge, feature_width), jnp.float32)
    )
    partial_rows = totals.reshape(row_tiles * tile_edge, feature_width)
    row_totals = lax.psum_scatter(
        partial_rows.astype(jnp.bfloat16), "col", scatter_dimension=0, tiled=True
    )
    hidden = jnp.dot(row_totals, weight, preferred_element_type=jnp.float32) + bias
    return jnp.maximum(hidden, 0.0).astype(jnp.bfloat16)


def solution(mesh):
    in_specs = (
        P(("row", "col"), None),
        P(("row", "col")),
        P("row", "col", None, None, None),
        P("row", "col", None, None),
        P("row", "col"),
        P(),
        P(),
    )
    out_specs = P(("row", "col"), None)
    return jax.shard_map(body, mesh=mesh, in_specs=in_specs, out_specs=out_specs, check_vma=False)
```

profile of v0, /device:TPU:0, one launch (start us, length us, event | category | flops | bytes accessed | tf_op | source)
XLA Modules:
  0.0 434.0 jit_solution(357774305717248672)
XLA Ops:
  6.5 0.0 copy-start
  6.5 0.0 copy-start.4
  6.5 0.0 copy-start.2
  6.5 0.7 compare_select_fusion.4
  7.3 0.1 copy.13
  7.4 0.3 fusion.10
  7.8 0.1 broadcast_add_fusion
  7.9 0.3 copy.14
  8.2 0.6 fusion.9
  8.9 0.0 copy-done.4
  8.9 0.1 and_reduce_fusion
  9.0 0.0 copy-done.2
  9.0 0.0 copy-done.3
  9.0 0.1 multiply_reduce_fusion
  9.1 8.1 %scatter_custom_fusion.2 = s32[4096]{0:T(1024)S(1)} fusion(s32[2048]{0:T(1024)S(1)} %get-tuple-element.68, s32[2048]{0:T(1024)S(1)} %get-tuple-element.66, s32[]{:T(128)} %constant.93.clone.1), kind=kCustom, calls=%fused_computation.54 | custom fusion | bytes 16388
  17.2 0.7 copy.15
  17.9 11.1 %all-to-all-start = ((s32[128,1,32]{2,1,0:T(1,128)}), s32[128,1,32]{2,1,0:T(1,128)S(1)}, u32[]{:S(2)}, u32[]{:S(2)}) async-start(s32[128,1,32]{2,1,0:T(1,128)} %copy.15), calls=%async_computation | async-start | bytes 131072 | tf_op jit(solution)/shard_map/all_to_all | solution.py:35
  29.1 7.1 %scatter_custom_fusion.3 = bf16[4096,128]{1,0:T(8,128)(2,1)} fusion(s32[2048]{0:T(1024)S(1)} %get-tuple-element.67, bf16[2048,128]{1,0:T(8,128)(2,1)} %param.9, bf16[]{:T(256)} %constant.92.clone.1), kind=kCustom, calls=%fused_computation.28 | custom fusion | bytes 1049088
  36.2 2.3 all-to-all-done
  38.5 7.4 %all-to-all-start.1 = ((bf16[128,32,128]{2,1,0:T(8,128)(2,1)}), bf16[128,32,128]{2,1,0:T(8,128)(2,1)S(1)}, u32[]{:S(2)}, u32[]{:S(2)}) async-start(bf16[128,32,128]{2,1,0:T(8,128)(2,1)} %bitcast.17), calls=%async_computation.1 | async-start | bytes 2097152 | tf_op jit(solution)/shard_map/all_to_all | solution.py:34
  46.0 0.0 all-gather.2.cloned.1.call-start
  46.0 0.6 broadcast.174
  46.6 0.8 reduce.10
  47.5 0.1 reshape.136
  47.6 17.4 %all-to-all-done.1 = bf16[128,32,128]{2,1,0:T(8,128)(2,1)S(1)} async-done(((bf16[128,32,128]{2,1,0:T(8,128)(2,1)}), bf16[128,32,128]{2,1,0:T(8,128)(2,1)S(1)}, u32[]{:S(2)}, u32[]{:S(2)}) %all-to-all-start.1) | async-done | bytes 1048608 | tf_op jit(solution)/shard_map/all_to_all | solution.py:34
  65.0 11.6 %scatter_custom_fusion.1 = bf16[2048,128]{1,0:T(8,128)(2,1)} fusion(s32[4096]{0:T(1024)S(1)} %bitcast.65, bf16[4096,128]{1,0:T(8,128)(2,1)S(1)} %bitcast.58, bf16[]{:T(256)} %constant.92.clone.1), kind=kCustom, calls=%fused_computation.32 | custom fusion | bytes 524290 | tf_op jit(solution)/shard_map/scatter | solution.py:40
  76.6 0.0 all-gather.2.cloned.1.call-update
  76.6 0.0 reduce-scatter.2.cloned.1.call-start
  77.3 27.0 %all-gather.2.cloned.1.call-done = bf16[16384,128]{1,0:T(8,128)(2,1)} async-done(((bf16[2048,128]{1,0:T(8,128)(2,1)}), bf16[16384,128]{1,0:T(8,128)(2,1)}) %all-gather.2.cloned.1.call-update) | async-done | bytes 4194320 | tf_op jit(solution)/shard_map/all_gather | solution.py:42
  104.4 7.8 %broadcast_in_dim.15 = f32[256,128,128]{2,1,0:T(8,128)} broadcast(f32[]{:T(128)} %constant.87.clone.1), dimensions={} | broadcast | bytes 16777220 | tf_op jit(solution)/shard_map/broadcast_in_dim | solution.py:66
  112.2 0.0 copy-done.1
  112.2 43.7 %while.10 = (s32[]{:T(128)}, f32[256,128,128]{2,1,0:T(8,128)}, s32[]{:T(128)}, s32[2,640]{1,0:T(2,128)S(1)}, s32[]{:T(128)}, /*index=5*/bf16[640,128,128]{2,1,0:...) while((s32[]{:T(128)}, f32[256,128,128]{2,1,0:T(8,128)}, ...), condition=%wide.region_8.9_spmd, body=%wide.region_6.8_spmd.sunk | while | flops 270534144 | bytes 25182252 | solution.py:65
  112.2 0.7 add_compare_fusion.2
  112.9 0.1 fusion.39
  113.0 3.1 gather_fusion
  116.1 4.3 convolution_select_fusion.2
  120.4 13.7 %scatter_fusion = f32[256,128,128]{2,1,0:T(8,128)} fusion(f32[256,128,128]{2,1,0:T(8,128)} %get-tuple-element.133, s32[64]{0:T(128)S(1)} %get-tuple-element.119, f32[64,128,128]{2,1,0:T(8,128)} %convolution_select_fusion.2), kind=kCustom, calls=%fused_computation.1.clone.1 | custom fusion | flops 1048576 | bytes 12583168 | tf_op jit(solution)/shard_map/while/body/scatter-add | solution.py:62
  134.1 0.7 add_compare_fusion.2
  134.8 0.1 fusion.39
  134.9 3.1 gather_fusion
  138.0 4.3 convolution_select_fusion.2
  142.3 13.7 %scatter_fusion = f32[256,128,128]{2,1,0:T(8,128)} fusion(f32[256,128,128]{2,1,0:T(8,128)} %get-tuple-element.133, s32[64]{0:T(128)S(1)} %get-tuple-element.119, f32[64,128,128]{2,1,0:T(8,128)} %convolution_select_fusion.2), kind=kCustom, calls=%fused_computation.1.clone.1 | custom fusion | flops 1048576 | bytes 12583168 | tf_op jit(solution)/shard_map/while/body/scatter-add | solution.py:62
  155.9 9.2 %convert_element_type.18 = bf16[256,128,128]{2,1,0:T(8,128)(2,1)} convert(f32[256,128,128]{2,1,0:T(8,128)} %get-tuple-element.43) | non-fusion elementwise | flops 4194304 | bytes 25165824 | tf_op jit(solution)/shard_map/convert_element_type | solution.py:70
  165.1 0.0 reduce-scatter.2.cloned.1.call-update
  165.2 259.5 %reduce-scatter.2.cloned.1.call-done = bf16[2048,128]{1,0:T(8,128)(2,1)} async-done(((bf16[32768,128]{1,0:T(8,128)(2,1)}), bf16[2048,128]{1,0:T(8,128)(2,1)}) %reduce-scatter.2.cloned.1.call-update) | async-done | bytes 524304 | tf_op jit(solution)/shard_map/reduce_scatter | solution.py:69
  424.7 0.0 copy-done
  424.7 0.0 copy-done.5
  424.7 2.4 fusion.7
  (13 shorter events, 0.1 us)
Async XLA Ops:
  6.5 418.2 %copy-start = (bf16[128,256]{1,0:T(8,128)(2,1)S(1)}, bf16[128,256]{1,0:T(8,128)(2,1)}, u32[]{:S(2)}) copy-start(bf16[128,256]{1,0:T(8,128)(2,1)} %param.14) | copy-start | bytes 196612
  6.5 2.3 copy-start.4
  6.5 2.4 copy-start.2
  6.5 2.5 copy-start.3
  17.9 20.6 %all-to-all-start = ((s32[128,1,32]{2,1,0:T(1,128)}), s32[128,1,32]{2,1,0:T(1,128)S(1)}, u32[]{:S(2)}, u32[]{:S(2)}) async-start(s32[128,1,32]{2,1,0:T(1,128)} %copy.15), calls=%async_computation | async-start | bytes 131072 | tf_op jit(solution)/shard_map/all_to_all | solution.py:35
  38.5 26.5 %all-to-all-start.1 = ((bf16[128,32,128]{2,1,0:T(8,128)(2,1)}), bf16[128,32,128]{2,1,0:T(8,128)(2,1)S(1)}, u32[]{:S(2)}, u32[]{:S(2)}) async-start(bf16[128,32,128]{2,1,0:T(8,128)(2,1)} %bitcast.17), calls=%async_computation.1 | async-start | bytes 2097152 | tf_op jit(solution)/shard_map/all_to_all | solution.py:34
  46.0 58.4 %all-gather.2.cloned.1.call-start = ((), (), s32[]{:S(2)}) async-start(), calls=%async_computation.3 | async-start | bytes 4718592 | tf_op jit(solution)/shard_map/all_gather | solution.py:42
  76.6 348.1 %reduce-scatter.2.cloned.1.call-start = ((), (), s32[]{:S(2)}) async-start(), calls=%async_computation.4 | async-start | bytes 8912896 | tf_op jit(solution)/shard_map/reduce_scatter | solution.py:69
  104.4 7.9 %copy-start.1 = (s32[1,1,2,640]{3,2,1,0:T(2,128)S(1)}, s32[1,1,2,640]{3,2,1,0:T(2,128)}, u32[]{:S(2)}) copy-start(s32[1,1,2,640]{3,2,1,0:T(2,128)} %param.12) | copy-start | bytes 15364
  165.1 259.6 %copy-start.5 = (f32[256]{0:T(256)S(1)}, f32[256]{0:T(256)}, u32[]{:S(2)}) copy-start(f32[256]{0:T(256)} %param.15) | copy-start | bytes 3076
Sparse Core Ops, SparseCore 0:
  76.8 27.5 all-gather.1
  165.3 259.3 reduce-scatter.1
where the time goes:
time: 436 us; the launch traced here: 434 us
  waiting for transfers between devices  306 us (70%)
  local copies, waits for them, and re-layouts  42.8 us (10%)
  other arithmetic  41 us (9%)
  starting transfers between devices  18.7 us (4%)
  between operations  14.2 us (3%)
  matrix products  11 us (3%)
    reduce_scatter x1, waiting for transfers between devices, body(): lax.psum_scatter(partial_rows.astype(jnp.bfloat16), 'col', scatter_dimens...  260 us
    scatter-add x2, other arithmetic, add_tiles(): return totals.at[part_rows].add(products)  27.4 us
    all_gather x1, waiting for transfers between devices, body(): column_block = lax.all_gather(moved_rows, 'row', axis=0, tiled=True)  27 us
    all_to_all x1, waiting for transfers between devices, body(): lax.all_to_all(outgoing, ('row', 'col'), split_axis=0, concat_axis=0, til...  17.4 us
    unnamed x14, local copies, waits for them, and re-layouts  15.2 us
    scatter x1, local copies, waits for them, and re-layouts, body(): moved_rows = jnp.zeros((local_rows, feature_width), jnp.bfloat16).at[slot...  11.6 us
    all_to_all x1, starting transfers between devices, body(): lax.all_to_all(slots_out, ('row', 'col'), split_axis=0, concat_axis=0, ti...  11.1 us
    convert_element_type x1, other arithmetic, body(): partial_rows.astype(jnp.bfloat16)  9.2 us
  transfers between devices with their start and end apart: 4, of which 4 were waited for; matrix products, arithmetic and copies ran while one was open for 2% of the time, Pallas kernels for 0%

commit v1 on v0

--- a/solution.py
+++ b/solution.py
@@ -2,8 +2,25 @@
 import jax.numpy as jnp
 from jax import lax
 from jax.sharding import PartitionSpec as P
+from jax.lax import axis_index, axis_size, ppermute
 
 GROUP = 64
+
+
+def try_all_the_axis_part(packet):
+    net_axis = "row"
+    cores_n = axis_size(net_axis)
+    found = tuple(((dev, (dev + 1) % cores_n) for dev in range(cores_n)))
+
+    def perform_the_slot(current_block):
+        if len(current_block) == cores_n:
+            return current_block
+        return perform_the_slot(
+            [ppermute(current_block[0], perm=found, axis_name=net_axis), *current_block]
+        )
+
+    z1 = jnp.concatenate(perform_the_slot([packet]), axis=0)
+    return jnp.roll(z1, (axis_index(net_axis) + 1) * packet.shape[0], axis=0)
 
 
 def body(features, new_index, tile_values, tile_index, tile_count, weight, bias):
@@ -39,7 +56,7 @@
         .at[slots_in.reshape(-1)]
         .set(rows_in.reshape(-1, feature_width), mode="drop")
     )
-    column_block = lax.all_gather(moved_rows, "row", axis=0, tiled=True)
+    column_block = try_all_the_axis_part(moved_rows)
     tile_set = tile_values[0, 0]
     tile_coords = tile_index[0, 0]
     tile_total = tile_count[0, 0]

time: 436 us -> 481 us (1.10)
  waiting for transfers between devices: 306 us -> 343 us
  local copies, waits for them, and re-layouts: 42.8 us -> 49.5 us
    ppermute x0 -> x7, waiting for transfers between devices: none -> 68.4 us  [perform_the_slot(): ppermute(current_block[0], perm=found, axis_name=net_axis)]
    all_gather x1 -> x0, waiting for transfers between devices: 27 us -> none  [body(): column_block = lax.all_gather(moved_rows, 'row', axis=0, tiled=True)]
    reduce_scatter x1, waiting for transfers between devices: 260 us -> 254 us  [body(): lax.psum_scatter(partial_rows.astype(jnp.bfloat16), 'col', scatter_dimens...]
    unnamed x14 -> x23, local copies, waits for them, and re-layouts: 15.2 us -> 20.4 us
  transfers between devices with their start and end apart: 4 -> 10, of which waited for: 4 -> 10; matrix products, arithmetic and copies ran while one was open for 2% -> 2% of each run, Pallas kernels for 0% -> 0%
where the time goes in v1:
time: 481 us; the launch traced here: 478 us
  waiting for transfers between devices  343 us (71%)
  local copies, waits for them, and re-layouts  49.5 us (10%)
  other arithmetic  42.3 us (9%)
  starting transfers between devices  18.7 us (4%)
  between operations  14.3 us (3%)
  matrix products  11 us (2%)
    reduce_scatter x1, waiting for transfers between devices, body(): lax.psum_scatter(partial_rows.astype(jnp.bfloat16), 'col', scatter_dimens...  254 us
    ppermute x7, waiting for transfers between devices, perform_the_slot(): ppermute(current_block[0], perm=found, axis_name=net_axis)  68.4 us
    scatter-add x2, other arithmetic, add_tiles(): return totals.at[part_rows].add(products)  27.4 us
    unnamed x23, local copies, waits for them, and re-layouts  20.4 us
    all_to_all x1, waiting for transfers between devices, body(): lax.all_to_all(outgoing, ('row', 'col'), split_axis=0, concat_axis=0, til...  17.4 us
    all_to_all x1, starting transfers between devices, body(): lax.all_to_all(slots_out, ('row', 'col'), split_axis=0, concat_axis=0, ti...  11.1 us
    scatter x1, local copies, waits for them, and re-layouts, body(): moved_rows = jnp.zeros((local_rows, feature_width), jnp.bfloat16).at[slot...  10.9 us
  transfers between devices with their start and end apart: 10, of which 10 were waited for; matrix products, arithmetic and copies ran while one was open for 2% of the time, Pallas kernels for 0%

profile of v1, /device:TPU:0, one launch (start us, length us, event | category | flops | bytes accessed | tf_op | source)
XLA Modules:
  0.0 478.3 jit_solution(16111796767804228149)
XLA Ops:
  6.5 0.8 compare_select_fusion.4
  7.3 0.1 copy.13
  7.4 0.3 fusion.10
  7.8 0.1 broadcast_add_fusion
  7.9 0.3 copy.14
  8.2 0.6 fusion.9
  8.9 0.8 and_reduce_fusion
  9.6 0.8 multiply_reduce_fusion
  10.4 8.1 %scatter_custom_fusion.2 = s32[4096]{0:T(1024)S(1)} fusion(s32[2048]{0:T(1024)S(1)} %get-tuple-element.68, s32[2048]{0:T(1024)S(1)} %get-tuple-element.66, s32[]{:T(128)} %constant.115.clone.1), kind=kCustom, calls=%fused_computation.70 | custom fusion | bytes 16388
  18.5 0.7 copy.15
  19.2 11.1 %all-to-all-start = ((s32[128,1,32]{2,1,0:T(1,128)}), s32[128,1,32]{2,1,0:T(1,128)S(1)}, u32[]{:S(2)}, u32[]{:S(2)}) async-start(s32[128,1,32]{2,1,0:T(1,128)} %copy.15), calls=%async_computation | async-start | bytes 131072 | tf_op jit(solution)/shard_map/all_to_all | solution.py:52
  30.4 7.1 %scatter_custom_fusion.3 = bf16[4096,128]{1,0:T(8,128)(2,1)} fusion(s32[2048]{0:T(1024)S(1)} %get-tuple-element.67, bf16[2048,128]{1,0:T(8,128)(2,1)} %param.9, bf16[]{:T(256)} %constant.114.clone.1), kind=kCustom, calls=%fused_computation.28 | custom fusion | bytes 1049088
  37.5 2.3 all-to-all-done
  39.8 7.4 %all-to-all-start.1 = ((bf16[128,32,128]{2,1,0:T(8,128)(2,1)}), bf16[128,32,128]{2,1,0:T(8,128)(2,1)S(1)}, u32[]{:S(2)}, u32[]{:S(2)}) async-start(bf16[128,32,128]{2,1,0:T(8,128)(2,1)} %bitcast.17), calls=%async_computation.1 | async-start | bytes 2097152 | tf_op jit(solution)/shard_map/all_to_all | solution.py:51
  47.3 0.6 broadcast.175
  47.9 0.8 reduce.10
  48.8 0.1 reshape.136
  48.9 17.4 %all-to-all-done.1 = bf16[128,32,128]{2,1,0:T(8,128)(2,1)S(1)} async-done(((bf16[128,32,128]{2,1,0:T(8,128)(2,1)}), bf16[128,32,128]{2,1,0:T(8,128)(2,1)S(1)}, u32[]{:S(2)}, u32[]{:S(2)}) %all-to-all-start.1) | async-done | bytes 1048608 | tf_op jit(solution)/shard_map/all_to_all | solution.py:51
  66.3 10.9 %scatter_custom_fusion.1 = bf16[2048,128]{1,0:T(8,128)(2,1)S(1)} fusion(s32[4096]{0:T(1024)S(1)} %bitcast.65, bf16[4096,128]{1,0:T(8,128)(2,1)S(1)} %bitcast.58, bf16[]{:T(256)} %constant.114.clone.1), kind=kCustom, calls=%fused_computation.32 | custom fusion | bytes 524290 | tf_op jit(solution)/shard_map/scatter | solution.py:57
  77.3 9.8 %collective-permute-done = bf16[2048,128]{1,0:T(8,128)(2,1)S(1)} collective-permute-done((bf16[2048,128]{1,0:T(8,128)(2,1)S(1)}, bf16[2048,128]{1,0:T(8,128)(2,1)S(1)}, u32[]{:S(2)}, u32[]{:S(2)}) %collective-permute-start) | collective-permute-done | bytes 524320 | tf_op jit(solution)/shard_map/ppermute | solution.py:19
  87.1 9.8 %collective-permute-done.1 = bf16[2048,128]{1,0:T(8,128)(2,1)S(1)} collective-permute-done((bf16[2048,128]{1,0:T(8,128)(2,1)S(1)}, bf16[2048,128]{1,0:T(8,128)(2,1)S(1)}, u32[]{:S(2)}, u32[]{:S(2)}) %collective-permute-start.1) | collective-permute-done | bytes 524320 | tf_op jit(solution)/shard_map/ppermute | solution.py:19
  96.9 9.8 %collective-permute-done.2 = bf16[2048,128]{1,0:T(8,128)(2,1)S(1)} collective-permute-done((bf16[2048,128]{1,0:T(8,128)(2,1)S(1)}, bf16[2048,128]{1,0:T(8,128)(2,1)S(1)}, u32[]{:S(2)}, u32[]{:S(2)}) %collective-permute-start.2) | collective-permute-done | bytes 524320 | tf_op jit(solution)/shard_map/ppermute | solution.py:19
  106.7 9.8 %collective-permute-done.3 = bf16[2048,128]{1,0:T(8,128)(2,1)S(1)} collective-permute-done((bf16[2048,128]{1,0:T(8,128)(2,1)S(1)}, bf16[2048,128]{1,0:T(8,128)(2,1)S(1)}, u32[]{:S(2)}, u32[]{:S(2)}) %collective-permute-start.3) | collective-permute-done | bytes 524320 | tf_op jit(solution)/shard_map/ppermute | solution.py:19
  116.5 9.8 %collective-permute-done.4 = bf16[2048,128]{1,0:T(8,128)(2,1)S(1)} collective-permute-done((bf16[2048,128]{1,0:T(8,128)(2,1)S(1)}, bf16[2048,128]{1,0:T(8,128)(2,1)S(1)}, u32[]{:S(2)}, u32[]{:S(2)}) %collective-permute-start.4) | collective-permute-done | bytes 524320 | tf_op jit(solution)/shard_map/ppermute | solution.py:19
  126.4 9.9 %collective-permute-done.5 = bf16[2048,128]{1,0:T(8,128)(2,1)} collective-permute-done((bf16[2048,128]{1,0:T(8,128)(2,1)S(1)}, bf16[2048,128]{1,0:T(8,128)(2,1)}, u32[]{:S(2)}, u32[]{:S(2)}) %collective-permute-start.5) | collective-permute-done | bytes 524320 | tf_op jit(solution)/shard_map/ppermute | solution.py:19
  137.0 9.4 %collective-permute-done.6 = bf16[2048,128]{1,0:T(8,128)(2,1)} collective-permute-done((bf16[2048,128]{1,0:T(8,128)(2,1)}, bf16[2048,128]{1,0:T(8,128)(2,1)}, u32[]{:S(2)}, u32[]{:S(2)}) %collective-permute-start.6) | collective-permute-done | bytes 524320 | tf_op jit(solution)/shard_map/ppermute | solution.py:19
  146.4 1.1 constant_dynamic-update-slice_fusion.15
  147.5 1.1 constant_dynamic-update-slice_fusion.14
  148.6 0.1 constant_dynamic-update-slice_fusion.13
  148.7 0.1 constant_dynamic-update-slice_fusion.12
  149.1 1.1 constant_dynamic-update-slice_fusion.7
  150.2 1.1 constant_dynamic-update-slice_fusion.6
  151.8 2.1 constant_dynamic-slice_fusion.2
  153.9 7.8 %broadcast_in_dim.15 = f32[256,128,128]{2,1,0:T(8,128)} broadcast(f32[]{:T(128)} %constant.109.clone.1), dimensions={} | broadcast | bytes 16777220 | tf_op jit(solution)/shard_map/broadcast_in_dim | solution.py:83
  161.7 43.7 %while.10 = (s32[]{:T(128)}, f32[256,128,128]{2,1,0:T(8,128)}, s32[]{:T(128)}, s32[2,640]{1,0:T(2,128)S(1)}, s32[]{:T(128)}, /*index=5*/bf16[640,128,128]{2,1,0:...) while((s32[]{:T(128)}, f32[256,128,128]{2,1,0:T(8,128)}, ...), condition=%wide.region_8.9_spmd, body=%wide.region_6.8_spmd.sunk | while | flops 270534144 | bytes 25182252 | solution.py:82
  161.7 0.7 add_compare_fusion.2
  162.4 0.1 fusion.39
  162.5 3.1 gather_fusion
  165.6 4.3 convolution_select_fusion.2
  169.9 13.7 %scatter_fusion = f32[256,128,128]{2,1,0:T(8,128)} fusion(f32[256,128,128]{2,1,0:T(8,128)} %get-tuple-element.133, s32[64]{0:T(128)S(1)} %get-tuple-element.119, f32[64,128,128]{2,1,0:T(8,128)} %convolution_select_fusion.2), kind=kCustom, calls=%fused_computation.1.clone.1 | custom fusion | flops 1048576 | bytes 12583168 | tf_op jit(solution)/shard_map/while/body/scatter-add | solution.py:79
  183.6 0.7 add_compare_fusion.2
  184.3 0.1 fusion.39
  184.3 3.1 gather_fusion
  187.5 4.3 convolution_select_fusion.2
  191.8 13.7 %scatter_fusion = f32[256,128,128]{2,1,0:T(8,128)} fusion(f32[256,128,128]{2,1,0:T(8,128)} %get-tuple-element.133, s32[64]{0:T(128)S(1)} %get-tuple-element.119, f32[64,128,128]{2,1,0:T(8,128)} %convolution_select_fusion.2), kind=kCustom, calls=%fused_computation.1.clone.1 | custom fusion | flops 1048576 | bytes 12583168 | tf_op jit(solution)/shard_map/while/body/scatter-add | solution.py:79
  205.4 9.2 %convert_element_type.18 = bf16[256,128,128]{2,1,0:T(8,128)(2,1)} convert(f32[256,128,128]{2,1,0:T(8,128)} %get-tuple-element.43) | non-fusion elementwise | flops 4194304 | bytes 25165824 | tf_op jit(solution)/shard_map/convert_element_type | solution.py:87
  214.7 254.3 %reduce-scatter.2.cloned.1.call-done = bf16[2048,128]{1,0:T(8,128)(2,1)} async-done(((bf16[32768,128]{1,0:T(8,128)(2,1)}), bf16[2048,128]{1,0:T(8,128)(2,1)}) %reduce-scatter.2.cloned.1.call-update) | async-done | bytes 524304 | tf_op jit(solution)/shard_map/reduce_scatter | solution.py:86
  469.0 2.4 fusion.7
  (35 shorter events, 0.9 us)
Async XLA Ops:
  6.5 462.4 %copy-start = (bf16[128,256]{1,0:T(8,128)(2,1)S(1)}, bf16[128,256]{1,0:T(8,128)(2,1)}, u32[]{:S(2)}) copy-start(bf16[128,256]{1,0:T(8,128)(2,1)} %param.14) | copy-start | bytes 196612
  19.2 20.6 %all-to-all-start = ((s32[128,1,32]{2,1,0:T(1,128)}), s32[128,1,32]{2,1,0:T(1,128)S(1)}, u32[]{:S(2)}, u32[]{:S(2)}) async-start(s32[128,1,32]{2,1,0:T(1,128)} %copy.15), calls=%async_computation | async-start | bytes 131072 | tf_op jit(solution)/shard_map/all_to_all | solution.py:52
  39.8 26.5 %all-to-all-start.1 = ((bf16[128,32,128]{2,1,0:T(8,128)(2,1)}), bf16[128,32,128]{2,1,0:T(8,128)(2,1)S(1)}, u32[]{:S(2)}, u32[]{:S(2)}) async-start(bf16[128,32,128]{2,1,0:T(8,128)(2,1)} %bitcast.17), calls=%async_computation.1 | async-start | bytes 2097152 | tf_op jit(solution)/shard_map/all_to_all | solution.py:51
  47.3 421.7 %reduce-scatter.2.cloned.1.call-start = ((), (), s32[]{:S(2)}) async-start(), calls=%async_computation.3 | async-start | bytes 8912896 | tf_op jit(solution)/shard_map/reduce_scatter | solution.py:86
  77.3 9.8 %collective-permute-start = (bf16[2048,128]{1,0:T(8,128)(2,1)S(1)}, bf16[2048,128]{1,0:T(8,128)(2,1)S(1)}, u32[]{:S(2)}, u32[]{:S(2)}) collective-permute-start(bf16[2048,128]{1,0:T(8,128)(2,1)S(1)} %scatter_custom_fusion.1), channel_id=1, source_target_pairs={{0,16},{16,32},{32,48},{48,64},{64,80},{80,96},{96,112},{112,0},{1... | collective-permute-start | bytes 1572872 | tf_op jit(solution)/shard_map/ppermute | solution.py:19
  87.1 9.8 %collective-permute-start.1 = (bf16[2048,128]{1,0:T(8,128)(2,1)S(1)}, bf16[2048,128]{1,0:T(8,128)(2,1)S(1)}, u32[]{:S(2)}, u32[]{:S(2)}) collective-permute-start(bf16[2048,128]{1,0:T(8,128)(2,1)S(1)} %collective-permute-done), channel_id=1, source_target_pairs={{0,16},{16,32},{32,48},{48,64},{64,80},{80,96},{96,112},{112,0},{1... | collective-permute-start | bytes 1572872 | tf_op jit(solution)/shard_map/ppermute | solution.py:19
  96.9 9.8 %collective-permute-start.2 = (bf16[2048,128]{1,0:T(8,128)(2,1)S(1)}, bf16[2048,128]{1,0:T(8,128)(2,1)S(1)}, u32[]{:S(2)}, u32[]{:S(2)}) collective-permute-start(bf16[2048,128]{1,0:T(8,128)(2,1)S(1)} %collective-permute-done.1), channel_id=1, source_target_pairs={{0,16},{16,32},{32,48},{48,64},{64,80},{80,96},{96,112},{112,0},{1... | collective-permute-start | bytes 1572872 | tf_op jit(solution)/shard_map/ppermute | solution.py:19
  106.7 9.8 %collective-permute-start.3 = (bf16[2048,128]{1,0:T(8,128)(2,1)S(1)}, bf16[2048,128]{1,0:T(8,128)(2,1)S(1)}, u32[]{:S(2)}, u32[]{:S(2)}) collective-permute-start(bf16[2048,128]{1,0:T(8,128)(2,1)S(1)} %collective-permute-done.2), channel_id=1, source_target_pairs={{0,16},{16,32},{32,48},{48,64},{64,80},{80,96},{96,112},{112,0},{1... | collective-permute-start | bytes 1572872 | tf_op jit(solution)/shard_map/ppermute | solution.py:19
  116.5 9.8 %collective-permute-start.4 = (bf16[2048,128]{1,0:T(8,128)(2,1)S(1)}, bf16[2048,128]{1,0:T(8,128)(2,1)S(1)}, u32[]{:S(2)}, u32[]{:S(2)}) collective-permute-start(bf16[2048,128]{1,0:T(8,128)(2,1)S(1)} %collective-permute-done.3), channel_id=1, source_target_pairs={{0,16},{16,32},{32,48},{48,64},{64,80},{80,96},{96,112},{112,0},{1... | collective-permute-start | bytes 1572872 | tf_op jit(solution)/shard_map/ppermute | solution.py:19
  126.4 9.9 %collective-permute-start.5 = (bf16[2048,128]{1,0:T(8,128)(2,1)S(1)}, bf16[2048,128]{1,0:T(8,128)(2,1)}, u32[]{:S(2)}, u32[]{:S(2)}) collective-permute-start(bf16[2048,128]{1,0:T(8,128)(2,1)S(1)} %collective-permute-done.4), channel_id=1, source_target_pairs={{0,16},{16,32},{32,48},{48,64},{64,80},{80,96},{96,112},{112,0},{1... | collective-permute-start | bytes 1572872 | tf_op jit(solution)/shard_map/ppermute | solution.py:19
  136.3 10.1 %collective-permute-start.6 = (bf16[2048,128]{1,0:T(8,128)(2,1)}, bf16[2048,128]{1,0:T(8,128)(2,1)}, u32[]{:S(2)}, u32[]{:S(2)}) collective-permute-start(bf16[2048,128]{1,0:T(8,128)(2,1)} %collective-permute-done.5), channel_id=1, source_target_pairs={{0,16},{16,32},{32,48},{48,64},{64,80},{80,96},{96,112},{112,0},{1... | collective-permute-start | bytes 1572872 | tf_op jit(solution)/shard_map/ppermute | solution.py:19
  153.9 7.9 %copy-start.1 = (s32[1,1,2,640]{3,2,1,0:T(2,128)S(1)}, s32[1,1,2,640]{3,2,1,0:T(2,128)}, u32[]{:S(2)}) copy-start(s32[1,1,2,640]{3,2,1,0:T(2,128)} %param.12) | copy-start | bytes 15364
  214.6 254.3 %copy-start.2 = (f32[256]{0:T(256)S(1)}, f32[256]{0:T(256)}, u32[]{:S(2)}) copy-start(f32[256]{0:T(256)} %param.15) | copy-start | bytes 3076
Sparse Core Ops, SparseCore 0:
  214.8 254.1 reduce-scatter.1
